TPU v7x, 32 devices: a whole 2x2x4 slice. The times are simulated.
32 devices in a mesh: runs: 2 (over y), ctx: 4 (over z), head: 4 (over x, core).
Axes of the slice: x: 2, y: 2, z: 4, core: 2. Of those that a mesh axis runs over, the one named last changes fastest.
Arguments:
- tokens: bfloat16 [4096, 2048], P(('runs', 'ctx', 'head')), parts along dimension 0, may hold values from -400 to 400
- in_gain: float32 [2048], replicated, may hold values from 0.1 to 1.9
- projections: bfloat16 [3, 2048, 2048], P(None, 'ctx', 'head'), may hold values from -0.125 to 0.125
- prior_state: float32 [32, 128, 128], P(('runs', 'head')), parts along dimension 0, may hold values from -256 to 256
- out_gain: float32 [2048], P('head'), may hold values from 0.1 to 1.9
Outputs:
- attended: bfloat16 [4096, 2048], P(('runs', 'ctx', 'head')), parts along dimension 0
There are 2 independent parts, one for each index of `runs`. A program takes and returns all parts, laid end to end along the dimension named above; an argument that names none is the same for every part. Nothing has to cross between parts.
All inputs are finite; a program needn't handle non-finite values.
Results may differ from a plain program's by a relative error of at most 0.0071.
Values may be sent and summed in bfloat16 or wider, within the bound.
A program may use at most 64 MiB of HBM per device.

v0:
```python
import jax
import jax.numpy as jnp
from jax import lax
from jax.sharding import PartitionSpec as P

BLOCK = 512


def prefix(part, axis, combine, identity):
    place = lax.axis_index(axis)
    gathered = lax.all_gather(part, axis)
    state = jnp.zeros_like(part) + jnp.asarray(identity, part.dtype)

    def one(step, state):
        return combine(state, lax.dynamic_index_in_dim(gathered, step, 0, False))

    return lax.fori_loop(0, place, one, state)


def rms_tokens(values_in, gain):
    wide = values_in.astype(jnp.float32)
    scale = lax.rsqrt(jnp.mean(wide * wide, axis=-1, keepdims=True) + 1e-06)
    return (wide * scale * gain).astype(jnp.bfloat16)


def combine_sum(earlier, later):
    return earlier + later


def on_device(tokens, in_gain, projections, prior_state, out_gain):
    normed = rms_tokens(tokens, in_gain)
    width_here = projections.shape[2]
    heads_here = prior_state.shape[0]
    head_dim = prior_state.shape[1]
    full_weights = lax.all_gather(projections, "ctx", axis=1, tiled=True)
    mapped = jnp.einsum(
        "td,jdc->jtc",
        lax.all_gather(normed, "head", axis=0, tiled=True),
        full_weights,
        preferred_element_type=jnp.float32,
    ).astype(jnp.bfloat16)
    span_rows = mapped.shape[1]
    blocks = span_rows // BLOCK
    shaped = mapped.reshape(3, blocks, BLOCK, heads_here, head_dim)
    queries = shaped[0]
    keys_all = shaped[1]
    values_all = shaped[2]
    block_states = jnp.einsum(
        "bkhd,bkhe->bhde", keys_all, values_all, preferred_element_type=jnp.float32
    )
    local_total = jnp.sum(block_states, axis=0)
    before = prefix(local_total, "ctx", combine_sum, jnp.zeros_like(local_total))
    entering = prior_state + before
    starts = entering[None] + jnp.cumsum(block_states, axis=0) - block_states
    position = jnp.arange(BLOCK, dtype=jnp.int32)
    causal = position[:, None] >= position[None, :]
    scores = jnp.einsum("bqhd,bkhd->bhqk", queries, keys_all, preferred_element_type=jnp.float32)
    scores = jnp.where(causal[None, None], scores, 0.0).astype(jnp.bfloat16)
    intra = jnp.einsum("bhqk,bkhd->bqhd", scores, values_all, preferred_element_type=jnp.float32)
    inter = jnp.einsum(
        "bqhd,bhde->bqhe", queries, starts.astype(jnp.bfloat16), preferred_element_type=jnp.float32
    )
    mixed = intra + inter
    scale = lax.rsqrt(jnp.mean(mixed * mixed, axis=-1, keepdims=True) + 1e-06)
    gains = out_gain.reshape(heads_here, head_dim)
    result = (mixed * scale * gains).astype(jnp.bfloat16).reshape(span_rows, width_here)
    return lax.all_to_all(result, "head", split_axis=0, concat_axis=1, tiled=True)


def solution(mesh):
    in_specs = (
        P(("runs", "ctx", "head"), None),
        P(),
        P(None, "ctx", "head"),
        P(("runs", "head"), None, None),
        P("head"),
    )
    out_specs = P(("runs", "ctx", "head"), None)
    return jax.shard_map(
        on_device, mesh=mesh, in_specs=in_specs, out_specs=out_specs, check_vma=False
    )
```

profile of v0, /device:TPU:0, one launch (start us, length us, event | category | flops | bytes accessed | tf_op | source)
XLA Modules:
  0.0 211.0 jit_solution(1581802129097191559)
XLA Ops:
  6.5 0.0 copy-start.1
  6.5 0.0 all-gather.5.cloned.1.call-start
  6.5 1.3 fusion.11
  7.9 2.0 fusion.13
  9.9 0.0 all-gather.5.cloned.1.call-update
  9.9 0.0 all-gather.7.cloned.1.call-start
  10.0 0.0 copy-done.1
  10.0 1.6 copy.11
  11.6 0.0 all-gather.7.cloned.1.call-update
  11.6 0.0 all-gather.9.cloned.1.call-start
  11.7 23.7 %all-gather.5.cloned.1.call-done = bf16[512,2048]{1,0:T(8,128)(2,1)} async-done(((bf16[128,2048]{1,0:T(8,128)(2,1)}), bf16[512,2048]{1,0:T(8,128)(2,1)}) %all-gather.5.cloned.1.call-update) | async-done | bytes 2097168 | tf_op jit(solution)/shard_map/all_gather | solution.py:38
  35.4 117.0 %all-gather.7.cloned.1.call-done = bf16[3,2048,512]{1,2,0:T(8,128)(2,1)} async-done(((bf16[3,512,512]{1,2,0:T(8,128)(2,1)}), bf16[3,2048,512]{1,2,0:T(8,128)(2,1)}) %all-gather.7.cloned.1.call-update) | async-done | bytes 6291472 | tf_op jit(solution)/shard_map/all_gather | solution.py:35
  152.3 6.9 %fusion.6 = bf16[3,512,512]{1,2,0:T(8,128)(2,1)S(1)} fusion(bf16[3,2048,512]{1,2,0:T(8,128)(2,1)} %all-gather.7.cloned.1.call-done, bf16[512,2048]{1,0:T(8,128)(2,1)} %all-gather.5.cloned.1.call-done), kind=kOutput, calls=%fused_computation.6 | convolution fusion | flops 3222011904 | bytes 9961472 | tf_op jit(solution)/shard_map/td,jdc->jtc/dot_general | solution.py:36
  159.2 0.1 fusion.18
  159.4 1.0 fusion.19
  160.4 0.0 all-gather.9.cloned.1.call-update
  160.4 0.1 iota_compare_fusion
  160.5 26.2 %all-gather.9.cloned.1.call-done = f32[16,128,128]{2,1,0:T(8,128)} async-done(((f32[4,128,128]{2,1,0:T(8,128)}), f32[16,128,128]{2,1,0:T(8,128)}) %all-gather.9.cloned.1.call-update) | async-done | bytes 1048592 | tf_op jit(solution)/shard_map/all_gather | solution.py:11
  186.7 0.0 copy-start
  186.7 0.0 copy-start.2
  186.7 0.9 copy-done
  187.6 0.1 copy-done.2
  187.7 1.3 fusion.15
  189.0 0.0 copy-start.3
  189.0 2.6 %multiply_reduce_fusion = (f32[512,4]{0,1:T(4,128)S(1)}, f32[1,512,4,128]{1,3,2,0:T(8,128)S(1)}) fusion(f32[4,128,512]{2,1,0:T(8,128)} %fusion.15, bf16[512,4,128]{0,2,1:T(8,128)(2,1)S(1)} %bitcast.38, bf16[512,4,128]{0,2,1:T(8,128)(2,1)S(1)} %bitcast.42, bf16[512,4,128]{0,2,1:T(8,128)(2,1)S(1)} %bitcast.40, pred[512,512]{1,0:T(8,128)(4,1)S(1)} %iota_compare_fusion), kind=kOutput, calls=%fused_computation.15 | convolution fusion | flops 539752448 | bytes 3940352 | tf_op jit(solution)/shard_map/bhqk,bkhd->bqhd/dot_general | solution.py:59
  191.7 0.0 copy-done.3
  191.7 0.2 multiply_convert_fusion
  191.9 0.1 all_to_all.14
  192.0 0.1 copy.15
  192.1 11.4 %all_to_all.19 = bf16[4,128,512]{1,2,0:T(8,128)(2,1)S(1)} all-to-all(bf16[4,128,512]{1,2,0:T(8,128)(2,1)S(1)} %copy.15), channel_id=1, replica_groups=mesh['runs'=2,'ctx'=4,'head'=4] {'head'}, dimensions={0} | all-to-all | bytes 1048576 | tf_op jit(solution)/shard_map/all_to_all | solution.py:67
  203.5 1.0 copy.16
  (4 shorter events, 0.0 us)
Async XLA Ops:
  6.5 3.5 %copy-start.1 = (bf16[3,512,512]{2,1,0:T(8,128)(2,1)S(1)}, bf16[3,512,512]{2,1,0:T(8,128)(2,1)}, u32[]{:S(2)}) copy-start(bf16[3,512,512]{2,1,0:T(8,128)(2,1)} %param.9) | copy-start | bytes 4718596
  6.5 28.9 %all-gather.5.cloned.1.call-start = ((), (), s32[]{:S(2)}) async-start(), calls=%async_computation.1 | async-start | bytes 2621440 | tf_op jit(solution)/shard_map/all_gather | solution.py:38
  9.9 142.4 %all-gather.7.cloned.1.call-start = ((), (), s32[]{:S(2)}) async-start(), calls=%async_computation.2 | async-start | bytes 7864320 | tf_op jit(solution)/shard_map/all_gather | solution.py:35
  11.6 175.0 %all-gather.9.cloned.1.call-start = ((), (), s32[]{:S(2)}) async-start(), calls=%async_computation.3 | async-start | bytes 1310720 | tf_op jit(solution)/shard_map/all_gather | solution.py:11
  186.7 1.0 copy-start
  186.7 1.0 copy-start.2
  189.0 2.7 %copy-start.3 = (f32[512]{0:T(512)S(1)}, f32[512]{0:T(512)}, u32[]{:S(2)}) copy-start(f32[512]{0:T(512)} %param.11) | copy-start | bytes 6148
Sparse Core Ops, SparseCore 0:
  10.1 25.2 all-gather.4
  37.0 115.3 all-gather.6
  160.5 26.1 all-gather.8
where the time goes:
time: 211 us
  waiting for transfers between devices  167 us (79%)
  between operations  13.2 us (6%)
  matrix products  11.9 us (6%)
  blocking collectives  11.4 us (5%)
  local copies, waits for them, and re-layouts  3.93 us (2%)
  other arithmetic  3.62 us (2%)
    all_gather x1, waiting for transfers between devices, on_device(): full_weights = lax.all_gather(projections, 'ctx', axis=1, tiled=True)  117 us
    all_gather x1, waiting for transfers between devices, prefix(): gathered = lax.all_gather(part, axis)  26.2 us
    all_gather x1, waiting for transfers between devices, on_device(): lax.all_gather(normed, 'head', axis=0, tiled=True)  23.7 us
    all_to_all x1, blocking collectives, on_device(): lax.all_to_all(result, 'head', split_axis=0, concat_axis=1, tiled=True)  11.4 us
    dot_general x1, matrix products, on_device(): jnp.einsum('td,jdc->jtc', lax.all_gather(normed, 'head', axis=0, tiled=Tr...  6.89 us
  transfers between devices with their start and end apart: 3, of which 3 were waited for; matrix products, arithmetic and copies ran while one was open for 1% of the time, Pallas kernels for 0%

commit v1 on v0

--- a/solution.py
+++ b/solution.py
@@ -4,6 +4,32 @@
 from jax.sharding import PartitionSpec as P
 
 BLOCK = 512
+
+
+def on_each_block(array, axis, dim, work, out_dim):
+    size, index, extent = (lax.axis_size(axis), lax.axis_index(axis), array.shape[dim])
+    forward = [(i, (i + 1) % size) for i in range(size)]
+    behind = [(b, a) for a, b in forward]
+    lower, upper = (lax.ppermute(array, axis, forward), lax.ppermute(array, axis, behind))
+    made = work(array, index * extent)
+    length = made.shape[out_dim]
+    whole = jnp.zeros(
+        (*made.shape[:out_dim], size * length, *made.shape[out_dim + 1 :]), made.dtype
+    )
+
+    def put(whole, made, source):
+        return lax.dynamic_update_slice_in_dim(whole, made, source * length, axis=out_dim)
+
+    whole = put(whole, made, index)
+    for step in range(1, size // 2 + 1):
+        below, above = ((index - step) % size, (index + step) % size)
+        held = (lower, upper)
+        if step < size // 2:
+            lower, upper = (lax.ppermute(lower, axis, forward), lax.ppermute(upper, axis, behind))
+        whole = put(whole, work(held[0], below * extent), below)
+        if 2 * step < size:
+            whole = put(whole, work(held[1], above * extent), above)
+    return whole
 
 
 def prefix(part, axis, combine, identity):
@@ -33,11 +59,14 @@
     heads_here = prior_state.shape[0]
     head_dim = prior_state.shape[1]
     full_weights = lax.all_gather(projections, "ctx", axis=1, tiled=True)
-    mapped = jnp.einsum(
-        "td,jdc->jtc",
-        lax.all_gather(normed, "head", axis=0, tiled=True),
-        full_weights,
-        preferred_element_type=jnp.float32,
+    mapped = on_each_block(
+        normed,
+        "head",
+        0,
+        lambda part_2, start: jnp.einsum(
+            "td,jdc->jtc", part_2, full_weights, preferred_element_type=jnp.float32
+        ),
+        1,
     ).astype(jnp.bfloat16)
     span_rows = mapped.shape[1]
     blocks = span_rows // BLOCK

time: 211 us -> 194 us (0.919)
  waiting for transfers between devices: 167 us -> 140 us
  matrix products: 11.9 us -> 17.4 us
  starting transfers between devices: 0.09 us -> 5.05 us
    all_gather x1 -> x0, waiting for transfers between devices: 23.7 us -> none  [on_device(): lax.all_gather(normed, 'head', axis=0, tiled=True)]
    all_gather x1, waiting for transfers between devices: 117 us -> 103 us  [on_device(): full_weights = lax.all_gather(projections, 'ctx', axis=1, tiled=True)]
    ppermute x0 -> x3, waiting for transfers between devices: none -> 9.76 us  [the longest x1 9.75 us: on_each_block(): lax.ppermute(array, axis, forward)]
    dot_general x1 -> x4, matrix products: 6.89 us -> 12.5 us  [on_device(): jnp.einsum('td,jdc->jtc', part_2, full_weights, preferred_element_type=jn...]
    ppermute x0 -> x3, starting transfers between devices: none -> 5.01 us  [the longest x1 2.52 us: on_each_block(): lax.ppermute(lower, axis, forward)]
  transfers between devices with their start and end apart: 3 -> 5, of which waited for: 3 -> 3; matrix products, arithmetic and copies ran while one was open for 1% -> 6% of each run, Pallas kernels for 0% -> 0%
where the time goes in v1:
time: 194 us
  waiting for transfers between devices  140 us (72%)
  matrix products  17.4 us (9%)
  between operations  13.6 us (7%)
  blocking collectives  11.4 us (6%)
  starting transfers between devices  5.05 us (3%)
  local copies, waits for them, and re-layouts  4.4 us (2%)
    all_gather x1, waiting for transfers between devices, on_device(): full_weights = lax.all_gather(projections, 'ctx', axis=1, tiled=True)  103 us
    all_gather x1, waiting for transfers between devices, prefix(): gathered = lax.all_gather(part, axis)  26.2 us
    dot_general x4, matrix products, on_device(): jnp.einsum('td,jdc->jtc', part_2, full_weights, preferred_element_type=jn...  12.5 us
    all_to_all x1, blocking collectives, on_device(): lax.all_to_all(result, 'head', split_axis=0, concat_axis=1, tiled=True)  11.4 us
    ppermute x1, waiting for transfers between devices, on_each_block(): lax.ppermute(array, axis, forward)  9.75 us
  transfers between devices with their start and end apart: 5, of which 3 were waited for; matrix products, arithmetic and copies ran while one was open for 6% of the time, Pallas kernels for 0%

profile of v1, /device:TPU:0, one launch (start us, length us, event | category | flops | bytes accessed | tf_op | source)
XLA Modules:
  0.0 193.7 jit_solution(5936233142773895514)
XLA Ops:
  6.5 0.0 copy-start.2
  6.5 0.0 copy-start.4
  6.5 0.0 all-gather.4.cloned.1.call-start
  6.5 0.7 all-gather.4.cloned.1.call-update
  7.3 0.0 all-gather.6.cloned.1.call-start
  7.3 1.2 fusion.3
  8.5 0.0 copy-done.2
  8.6 0.0 copy-done.4
  8.6 0.2 fusion.5
  8.8 0.5 collective-permute-start
  9.3 2.0 %collective-permute-start.1 = (bf16[128,2048]{1,0:T(8,128)(2,1)S(1)}, bf16[128,2048]{1,0:T(8,128)(2,1)S(1)}, u32[]{:S(2)}, u32[]{:S(2)}) collective-permute-start(bf16[128,2048]{1,0:T(8,128)(2,1)S(1)} %fusion.5), channel_id=1, source_target_pairs={{1,0},{2,1},{3,2},{0,3},{5,4},{6,5},{7,6},{4,7},{9,8},{10,9},{11,1... | collective-permute-start | bytes 1572872 | tf_op jit(solution)/shard_map/ppermute | solution.py:13
  11.3 9.8 %collective-permute-done = bf16[128,2048]{1,0:T(8,128)(2,1)S(1)} collective-permute-done((bf16[128,2048]{1,0:T(8,128)(2,1)S(1)}, bf16[128,2048]{1,0:T(8,128)(2,1)S(1)}, u32[]{:S(2)}, u32[]{:S(2)}) %collective-permute-start) | collective-permute-done | bytes 524320 | tf_op jit(solution)/shard_map/ppermute | solution.py:13
  21.0 2.5 %collective-permute-start.2 = (bf16[128,2048]{1,0:T(8,128)(2,1)S(1)}, bf16[128,2048]{1,0:T(8,128)(2,1)S(1)}, u32[]{:S(2)}, u32[]{:S(2)}) collective-permute-start(bf16[128,2048]{1,0:T(8,128)(2,1)S(1)} %collective-permute-done), channel_id=1, source_target_pairs={{0,1},{1,2},{2,3},{3,0},{4,5},{5,6},{6,7},{7,4},{8,9},{9,10},{10,1... | collective-permute-start | bytes 1572872 | tf_op jit(solution)/shard_map/ppermute | solution.py:28
  23.5 103.5 %all-gather.4.cloned.1.call-done = bf16[3,2048,512]{2,1,0:T(8,128)(2,1)} async-done(((bf16[3,512,512]{2,1,0:T(8,128)(2,1)}), bf16[3,2048,512]{2,1,0:T(8,128)(2,1)}) %all-gather.4.cloned.1.call-update) | async-done | bytes 6291472 | tf_op jit(solution)/shard_map/all_gather | solution.py:61
  127.0 0.0 copy-start
  127.0 3.9 %convolution_bitcast_fusion.3 = bf16[3,128,512]{2,1,0:T(8,128)(2,1)S(1)} fusion(bf16[3,2048,512]{2,1,0:T(8,128)(2,1)} %all-gather.4.cloned.1.call-done, bf16[128,2048]{1,0:T(8,128)(2,1)S(1)} %fusion.5), kind=kOutput, calls=%fused_computation.10 | convolution fusion | flops 805306368 | bytes 7208960 | tf_op jit(solution)/shard_map/td,jdc->jtc/dot_general | solution.py:66
  130.9 0.0 collective-permute-done.1
  131.0 0.7 copy-done
  131.6 1.0 convolution_bitcast_fusion.1
  132.6 0.2 copy.33
  132.8 0.2 copy.35
  133.1 3.8 %convolution_bitcast_fusion.2 = bf16[3,128,512]{2,1,0:T(8,128)(2,1)S(1)} fusion(bf16[3,2048,512]{2,1,0:T(8,128)(2,1)} %all-gather.4.cloned.1.call-done, bf16[128,2048]{1,0:T(8,128)(2,1)S(1)} %collective-permute-done), kind=kOutput, calls=%fused_computation.9 | convolution fusion | flops 805306368 | bytes 7208960 | tf_op jit(solution)/shard_map/td,jdc->jtc/dot_general | solution.py:66
  136.9 0.2 copy.34
  137.1 0.0 collective-permute-done.2
  137.1 3.8 %convolution_bitcast_fusion = bf16[3,128,512]{2,1,0:T(8,128)(2,1)S(1)} fusion(bf16[3,2048,512]{2,1,0:T(8,128)(2,1)} %all-gather.4.cloned.1.call-done, bf16[128,2048]{1,0:T(8,128)(2,1)S(1)} %collective-permute-done.2), kind=kOutput, calls=%fused_computation.7 | convolution fusion | flops 805306368 | bytes 7208960 | tf_op jit(solution)/shard_map/td,jdc->jtc/dot_general | solution.py:66
  140.9 0.2 copy.36
  141.1 0.1 broadcast_in_dim.16
  141.2 0.1 constant_dynamic-update-slice_fusion.3
  141.3 0.1 constant_dynamic-update-slice_fusion.2
  141.4 0.1 constant_dynamic-update-slice_fusion.1
  141.6 0.1 constant_dynamic-update-slice_fusion
  141.7 0.1 fusion.14
  141.8 1.0 fusion.15
  142.8 0.0 all-gather.6.cloned.1.call-update
  142.8 0.1 iota_compare_fusion
  142.9 26.2 %all-gather.6.cloned.1.call-done = f32[16,128,128]{2,1,0:T(8,128)} async-done(((f32[4,128,128]{2,1,0:T(8,128)}), f32[16,128,128]{2,1,0:T(8,128)}) %all-gather.6.cloned.1.call-update) | async-done | bytes 1048592 | tf_op jit(solution)/shard_map/all_gather | solution.py:37
  169.1 0.0 copy-start.1
  169.1 0.0 copy-start.3
  169.1 0.9 copy-done.1
  170.1 0.1 copy-done.3
  170.1 1.3 fusion.11
  171.5 0.0 copy-start.5
  171.5 2.6 %multiply_reduce_fusion = (f32[512,4]{0,1:T(4,128)S(1)}, f32[1,512,4,128]{1,3,2,0:T(8,128)S(1)}) fusion(f32[4,128,512]{2,1,0:T(8,128)} %fusion.11, bf16[512,4,128]{0,2,1:T(8,128)(2,1)S(1)} %bitcast.52, bf16[512,4,128]{0,2,1:T(8,128)(2,1)S(1)} %bitcast.56, bf16[512,4,128]{0,2,1:T(8,128)(2,1)S(1)} %bitcast.54, pred[512,512]{1,0:T(8,128)(4,1)S(1)} %iota_compare_fusion), kind=kOutput, calls=%fused_computation.15 | convolution fusion | flops 539752448 | bytes 3940352 | tf_op jit(solution)/shard_map/bhqk,bkhd->bqhd/dot_general | solution.py:88
  174.1 0.0 copy-done.5
  174.1 0.2 multiply_convert_fusion
  174.3 0.1 all_to_all.14
  174.4 0.1 copy.42
  174.5 11.4 %all_to_all.19 = bf16[4,128,512]{1,2,0:T(8,128)(2,1)S(1)} all-to-all(bf16[4,128,512]{1,2,0:T(8,128)(2,1)S(1)} %copy.42), channel_id=1, replica_groups=mesh['runs'=2,'ctx'=4,'head'=4] {'head'}, dimensions={0} | all-to-all | bytes 1048576 | tf_op jit(solution)/shard_map/all_to_all | solution.py:96
  185.9 1.0 copy.43
  (4 shorter events, 0.0 us)
Async XLA Ops:
  6.5 2.0 %copy-start.2 = (bf16[128,2048]{1,0:T(8,128)(2,1)S(1)}, bf16[128,2048]{1,0:T(8,128)(2,1)}, u32[]{:S(2)}) copy-start(bf16[128,2048]{1,0:T(8,128)(2,1)} %param.7) | copy-start | bytes 1572868
  6.5 2.0 %copy-start.4 = (f32[2048]{0:T(1024)S(1)}, f32[2048]{0:T(1024)}, u32[]{:S(2)}) copy-start(f32[2048]{0:T(1024)} %param.8) | copy-start | bytes 24580
  6.5 120.5 %all-gather.4.cloned.1.call-start = ((), (), s32[]{:S(2)}) async-start(), calls=%async_computation.1 | async-start | bytes 7864320 | tf_op jit(solution)/shard_map/all_gather | solution.py:61
  7.3 161.8 %all-gather.6.cloned.1.call-start = ((), (), s32[]{:S(2)}) async-start(), calls=%async_computation.2 | async-start | bytes 1310720 | tf_op jit(solution)/shard_map/all_gather | solution.py:37
  8.8 12.2 %collective-permute-start = (bf16[128,2048]{1,0:T(8,128)(2,1)S(1)}, bf16[128,2048]{1,0:T(8,128)(2,1)S(1)}, u32[]{:S(2)}, u32[]{:S(2)}) collective-permute-start(bf16[128,2048]{1,0:T(8,128)(2,1)S(1)} %fusion.5), channel_id=1, source_target_pairs={{0,1},{1,2},{2,3},{3,0},{4,5},{5,6},{6,7},{7,4},{8,9},{9,10},{10,1... | collective-permute-start | bytes 1572872 | tf_op jit(solution)/shard_map/ppermute | solution.py:13
  9.3 121.7 %collective-permute-start.1 = (bf16[128,2048]{1,0:T(8,128)(2,1)S(1)}, bf16[128,2048]{1,0:T(8,128)(2,1)S(1)}, u32[]{:S(2)}, u32[]{:S(2)}) collective-permute-start(bf16[128,2048]{1,0:T(8,128)(2,1)S(1)} %fusion.5), channel_id=1, source_target_pairs={{1,0},{2,1},{3,2},{0,3},{5,4},{6,5},{7,6},{4,7},{9,8},{10,9},{11,1... | collective-permute-start | bytes 1572872 | tf_op jit(solution)/shard_map/ppermute | solution.py:13
  21.0 116.1 %collective-permute-start.2 = (bf16[128,2048]{1,0:T(8,128)(2,1)S(1)}, bf16[128,2048]{1,0:T(8,128)(2,1)S(1)}, u32[]{:S(2)}, u32[]{:S(2)}) collective-permute-start(bf16[128,2048]{1,0:T(8,128)(2,1)S(1)} %collective-permute-done), channel_id=1, source_target_pairs={{0,1},{1,2},{2,3},{3,0},{4,5},{5,6},{6,7},{7,4},{8,9},{9,10},{10,1... | collective-permute-start | bytes 1572872 | tf_op jit(solution)/shard_map/ppermute | solution.py:28
  127.0 4.6 %copy-start = (bf16[3,2048,512]{2,1,0:T(8,128)(2,1)S(1)}, bf16[3,2048,512]{2,1,0:T(8,128)(2,1)}, u32[]{:S(2)}) copy-start(bf16[3,2048,512]{2,1,0:T(8,128)(2,1)} %all-gather.4.cloned.1.call-done) | copy-start | bytes 18874372
  169.1 1.0 copy-start.1
  169.1 1.0 copy-start.3
  171.5 2.7 %copy-start.5 = (f32[512]{0:T(512)S(1)}, f32[512]{0:T(512)}, u32[]{:S(2)}) copy-start(f32[512]{0:T(512)} %param.11) | copy-start | bytes 6148
Sparse Core Ops, SparseCore 0:
  8.9 118.0 all-gather.3
  142.9 26.1 all-gather.5
